TPU v7x, 32 devices: a whole 2x2x4 slice. The times are simulated.
32 devices in a mesh: replica: 4 (over x, core), fsdp: 8 (over z, y).
Axes of the slice: x: 2, y: 2, z: 4, core: 2. Of those that a mesh axis runs over, the one named last changes fastest.
Arguments:
- byte_input: bfloat16 [32768, 768], P(('replica', 'fsdp')), may hold values from -6 to 6
- global_out: bfloat16 [32768, 768], P(('replica', 'fsdp')), may hold values from -6 to 6
- cotangent: bfloat16 [32768, 768], P(('replica', 'fsdp')), may hold values from -6 to 6
- seq_patches: int32 [4, 4], P('replica'), may hold values from 1 to 512, 1024 in all within a row
- last_fill: int32 [4, 4], P('replica'), may hold values from 1 to 8
- deal_slots: int32 [4, 1024], P('replica', 'fsdp'), may hold values from 0 to 1023, as said below
- first_gain: bfloat16 [768], P('fsdp'), may hold values from 0.5 to 1.5
- first_shift: bfloat16 [768], P('fsdp'), may hold values from -1.796875 to 1.796875
- qkv_weight: bfloat16 [768, 2304], P('fsdp'), may hold values from -0.21875 to 0.21875
- out_weight: bfloat16 [768, 768], P('fsdp'), may hold values from -0.4375 to 0.4375
- second_gain: bfloat16 [768], P('fsdp'), may hold values from 0.5 to 1.5
- second_shift: bfloat16 [768], P('fsdp'), may hold values from -1.796875 to 1.796875
- up_weight: bfloat16 [768, 3072], P('fsdp'), may hold values from -0.21875 to 0.21875
- up_bias: bfloat16 [3072], P('fsdp'), may hold values from -3 to 3
- down_weight: bfloat16 [3072, 768], P('fsdp'), may hold values from -0.15625 to 0.15625
- down_bias: bfloat16 [768], P('fsdp'), may hold values from -1.796875 to 1.796875
Outputs:
- layer_out: bfloat16 [32768, 768], P(('replica', 'fsdp'))
- grad_input: bfloat16 [32768, 768], P(('replica', 'fsdp'))
- grad_global: bfloat16 [32768, 768], P(('replica', 'fsdp'))
- grad_first_gain: float32 [768], P('fsdp')
- grad_first_shift: float32 [768], P('fsdp')
- grad_qkv_weight: float32 [768, 2304], P('fsdp')
- grad_out_weight: float32 [768, 768], P('fsdp')
- grad_second_gain: float32 [768], P('fsdp')
- grad_second_shift: float32 [768], P('fsdp')
- grad_up_weight: float32 [768, 3072], P('fsdp')
- grad_up_bias: float32 [3072], P('fsdp')
- grad_down_weight: float32 [3072, 768], P('fsdp')
- grad_down_bias: float32 [768], P('fsdp')
Inputs may be any that keep to these rules, and one draw needn't show every extreme that they name: `seq_patches`: row g gives the patches of the 4 sequences of group g in order; each row sums to 1024 and its largest entry is 512. `last_fill`: bytes used in the last patch of each sequence; the rest of that patch is padding. Each row is a permutation of 0 to 1023. Of the patches p in any aligned block of 128, exactly 16 have deal_slots in each aligned block of 128 positions.
All inputs are finite; a program needn't handle non-finite values.
Results may differ from a plain program's by a relative error of at most 0.017.
Values may be sent and summed in bfloat16 or wider, within the bound.
No kernel may reach another device: no remote copies, remote signals or barrier semaphores. Data moves between devices by JAX's collectives and lax.ppermute only.
A program may use at most 128 MiB of HBM per device.

v0:
```python
import jax
import jax.numpy as jnp
from jax import lax
from jax.sharding import PartitionSpec as P

HEADS = 12
HEAD_DIM = 64
PATCH = 8
EPSILON = 1e-05


def contract_rows(left, right):
    return lax.dot_general(
        left, right, (((0,), (0,)), ((), ())), preferred_element_type=jnp.float32
    )


def contract_cols(left, right):
    return lax.dot_general(
        left, right, (((1,), (1,)), ((), ())), preferred_element_type=jnp.float32
    )


def apply_layer_normalize(values, gain, shift):
    center = values - jnp.mean(values, axis=1, keepdims=True)
    inverse = lax.rsqrt(jnp.mean(jnp.square(center), axis=1, keepdims=True) + EPSILON)
    normed = center * inverse
    return (normed * gain + shift, normed, inverse)


def normalize_pullback(upstream, gain, normed, inverse):
    scaled = upstream * gain
    inner = (
        scaled
        - jnp.mean(scaled, axis=1, keepdims=True)
        - normed * jnp.mean(scaled * normed, axis=1, keepdims=True)
    )
    return (inverse * inner, jnp.sum(upstream * normed, axis=0), jnp.sum(upstream, axis=0))


def block_mask(span):
    index = jnp.arange(span, dtype=jnp.int32)
    return (index[:, None] // PATCH == index[None, :] // PATCH) & (index[None, :] <= index[:, None])


def attention_scores(queries, keys_part, allowed):
    raw = jnp.einsum(
        "gqhd,gkhd->ghqk", queries, keys_part, preferred_element_type=jnp.float32
    ) * HEAD_DIM ** (-0.5)
    return jnp.where(allowed, raw, -1e30)


def body(
    byte_input,
    global_out,
    cotangent,
    seq_patches,
    last_fill,
    deal_slots,
    first_gain,
    first_shift,
    qkv_weight,
    out_weight,
    second_gain,
    second_shift,
    up_weight,
    up_bias,
    down_weight,
    down_bias,
):
    row_count = byte_input.shape[0]
    model_width = byte_input.shape[1]
    patch_count = row_count // PATCH
    fsdp_count = lax.axis_size("fsdp")
    share = patch_count // fsdp_count
    patch_ids = lax.axis_index("fsdp") * patch_count + jnp.arange(patch_count, dtype=jnp.int32)
    seq_ends = jnp.cumsum(seq_patches[0])
    seq_ids = jnp.sum((patch_ids[:, None] >= seq_ends[None, :]).astype(jnp.int32), axis=1)
    seq_hits = (seq_ids[:, None] == jnp.arange(seq_ends.shape[0], dtype=jnp.int32)[None, :]).astype(
        jnp.int32
    )
    end_of = jnp.sum(seq_hits * seq_ends[None, :], axis=1)
    fill_of = jnp.sum(seq_hits * last_fill[0][None, :], axis=1)
    in_patch = jnp.arange(PATCH, dtype=jnp.int32)
    keep_byte = (
        (patch_ids != end_of - 1)[:, None] | (in_patch[None, :] < fill_of[:, None])
    ).reshape(row_count, 1)
    target = deal_slots[0] // patch_count
    dealt_slot = deal_slots[0] % patch_count
    dest_hits = (target[:, None] == jnp.arange(fsdp_count, dtype=jnp.int32)[None, :]).astype(
        jnp.int32
    )
    dest_rank = jnp.sum((jnp.cumsum(dest_hits, axis=0) - 1) * dest_hits, axis=1)
    send_place = target * share + dest_rank
    send_order = (
        jnp.zeros((patch_count,), jnp.int32)
        .at[send_place]
        .set(jnp.arange(patch_count, dtype=jnp.int32))
    )

    def pack_rows(values):
        return values.reshape(patch_count, PATCH, model_width)[send_order].reshape(
            row_count, model_width
        )

    def unpack_rows(values):
        return values.reshape(patch_count, PATCH, model_width)[send_place].reshape(
            row_count, model_width
        )

    arrived, arrived_slot = (
        lax.all_to_all(pack_rows(byte_input), "fsdp", split_axis=0, concat_axis=0, tiled=True),
        lax.all_to_all(dealt_slot[send_order], "fsdp", split_axis=0, concat_axis=0, tiled=True),
    )
    (
        gain_full,
        complete_shift_vector,
        qkv_full,
        outproj_full,
        gain_later,
        deferred_shift_vector,
        expand_full,
        expand_bias,
        reduce_full,
        reduce_bias,
    ) = (
        lax.all_gather(first_gain, "fsdp", axis=0, tiled=True),
        lax.all_gather(first_shift, "fsdp", axis=0, tiled=True),
        lax.all_gather(qkv_weight, "fsdp", axis=0, tiled=True),
        lax.all_gather(out_weight, "fsdp", axis=0, tiled=True),
        lax.all_gather(second_gain, "fsdp", axis=0, tiled=True),
        lax.all_gather(second_shift, "fsdp", axis=0, tiled=True),
        lax.all_gather(up_weight, "fsdp", axis=0, tiled=True),
        lax.all_gather(up_bias, "fsdp", axis=0, tiled=True),
        lax.all_gather(down_weight, "fsdp", axis=0, tiled=True),
        lax.all_gather(down_bias, "fsdp", axis=0, tiled=True),
    )
    attention_norm_gain = gain_full.astype(jnp.float32)
    feedforward_norm_gain = gain_later.astype(jnp.float32)
    global_rows = global_out.reshape(patch_count, PATCH, model_width)[arrived_slot].reshape(
        row_count, model_width
    )
    residual_input = arrived.astype(jnp.float32) + global_rows.astype(jnp.float32)
    attention_normed_input, attention_centered_scaled, attention_inverse_deviation = (
        apply_layer_normalize(
            residual_input, attention_norm_gain, complete_shift_vector.astype(jnp.float32)
        )
    )
    first_in = attention_normed_input.astype(jnp.bfloat16)
    qkv_rows = jnp.dot(first_in, qkv_full, preferred_element_type=jnp.float32).astype(jnp.bfloat16)
    blocks = row_count // 128

    def heads_of(values, start):
        return lax.slice_in_dim(values, start, start + model_width, axis=1).reshape(
            blocks, 128, HEADS, HEAD_DIM
        )

    queries = heads_of(qkv_rows, 0)
    keys_part = heads_of(qkv_rows, model_width)
    values_part = heads_of(qkv_rows, 2 * model_width)
    allowed = block_mask(128)
    scores = attention_scores(queries, keys_part, allowed)
    top_score = jnp.max(scores, axis=3, keepdims=True)
    expo = jnp.exp(scores - top_score)
    total = jnp.sum(expo, axis=3, keepdims=True)
    log_total = top_score + jnp.log(total)
    probs = (expo / total).astype(jnp.bfloat16)
    mixed = jnp.einsum("ghqk,gkhd->gqhd", probs, values_part, preferred_element_type=jnp.float32)
    attended = mixed.reshape(row_count, model_width).astype(jnp.bfloat16)
    residual_midway = residual_input + jnp.dot(
        attended, outproj_full, preferred_element_type=jnp.float32
    )
    feedforward_normed_input, feedforward_centered_scaled, feedforward_inverse_deviation = (
        apply_layer_normalize(
            residual_midway, feedforward_norm_gain, deferred_shift_vector.astype(jnp.float32)
        )
    )
    second_in = feedforward_normed_input.astype(jnp.bfloat16)
    pre_act = jnp.dot(
        second_in, expand_full, preferred_element_type=jnp.float32
    ) + expand_bias.astype(jnp.float32)
    activ = jax.nn.gelu(pre_act, approximate=False).astype(jnp.bfloat16)
    result = (
        residual_midway
        + jnp.dot(activ, reduce_full, preferred_element_type=jnp.float32)
        + reduce_bias.astype(jnp.float32)
    )
    returned = lax.all_to_all(
        result.astype(jnp.bfloat16), "fsdp", split_axis=0, concat_axis=0, tiled=True
    )
    layer_out = jnp.where(keep_byte, unpack_rows(returned), jnp.zeros((), jnp.bfloat16))
    masked_cot = jnp.where(keep_byte, cotangent, jnp.zeros((), jnp.bfloat16))
    upstream_b = lax.all_to_all(
        pack_rows(masked_cot), "fsdp", split_axis=0, concat_axis=0, tiled=True
    )
    upstream = upstream_b.astype(jnp.float32)
    grad_reduce_bias = jnp.sum(upstream, axis=0)
    grad_reduce = contract_rows(activ, upstream_b)
    grad_activ = contract_cols(upstream_b, reduce_full)
    density = jnp.exp(-0.5 * jnp.square(pre_act)) * 0.3989422804014327
    cumulative = 0.5 * (1.0 + jax.scipy.special.erf(pre_act * 0.7071067811865476))
    grad_pre = (grad_activ * (cumulative + pre_act * density)).astype(jnp.bfloat16)
    grad_expand_bias = jnp.sum(grad_pre.astype(jnp.float32), axis=0)
    grad_expand = contract_rows(second_in, grad_pre)
    gradient_feedforward_branch = contract_cols(grad_pre, expand_full)
    normalize_piece, gradient_feedforward_gain, gradient_feedforward_shift = normalize_pullback(
        gradient_feedforward_branch,
        feedforward_norm_gain,
        feedforward_centered_scaled,
        feedforward_inverse_deviation,
    )
    grad_middle = upstream + normalize_piece
    grad_branch = grad_middle.astype(jnp.bfloat16)
    grad_outproj = contract_rows(attended, grad_branch)
    grad_attended = (
        contract_cols(grad_branch, outproj_full)
        .astype(jnp.bfloat16)
        .reshape(blocks, 128, HEADS, HEAD_DIM)
    )
    scores_again = attention_scores(queries, keys_part, allowed)
    probs_again = jnp.exp(scores_again - log_total)
    grad_probs = jnp.einsum(
        "gqhd,gkhd->ghqk", grad_attended, values_part, preferred_element_type=jnp.float32
    )
    grad_values = jnp.einsum(
        "ghqk,gqhd->gkhd",
        probs_again.astype(jnp.bfloat16),
        grad_attended,
        preferred_element_type=jnp.float32,
    )
    grad_scores = (
        probs_again * (grad_probs - jnp.sum(probs_again * grad_probs, axis=3, keepdims=True))
    ).astype(jnp.bfloat16)
    grad_queries = jnp.einsum(
        "ghqk,gkhd->gqhd", grad_scores, keys_part, preferred_element_type=jnp.float32
    ) * HEAD_DIM ** (-0.5)
    grad_keys = jnp.einsum(
        "ghqk,gqhd->gkhd", grad_scores, queries, preferred_element_type=jnp.float32
    ) * HEAD_DIM ** (-0.5)
    grad_qkv = jnp.concatenate(
        [
            grad_queries.reshape(row_count, model_width),
            grad_keys.reshape(row_count, model_width),
            grad_values.reshape(row_count, model_width),
        ],
        axis=1,
    ).astype(jnp.bfloat16)
    grad_qkv_full = contract_rows(first_in, grad_qkv)
    gradient_attention_branch = contract_cols(grad_qkv, qkv_full)
    normalize_before_attention, gradient_attention_gain, gradient_attention_shift = (
        normalize_pullback(
            gradient_attention_branch,
            attention_norm_gain,
            attention_centered_scaled,
            attention_inverse_deviation,
        )
    )
    grad_base = (grad_middle + normalize_before_attention).astype(jnp.bfloat16)
    inverse_slot = (
        jnp.zeros((patch_count,), jnp.int32)
        .at[arrived_slot]
        .set(jnp.arange(patch_count, dtype=jnp.int32))
    )
    grad_global = grad_base.reshape(patch_count, PATCH, model_width)[inverse_slot].reshape(
        row_count, model_width
    )
    sent_back = lax.all_to_all(grad_base, "fsdp", split_axis=0, concat_axis=0, tiled=True)
    grad_input = unpack_rows(sent_back)
    owned = (
        lax.psum_scatter(
            gradient_attention_gain.astype(jnp.bfloat16), "fsdp", scatter_dimension=0, tiled=True
        ).astype(jnp.float32),
        lax.psum_scatter(
            gradient_attention_shift.astype(jnp.bfloat16), "fsdp", scatter_dimension=0, tiled=True
        ).astype(jnp.float32),
        lax.psum_scatter(
            grad_qkv_full.astype(jnp.bfloat16), "fsdp", scatter_dimension=0, tiled=True
        ).astype(jnp.float32),
        lax.psum_scatter(
            grad_outproj.astype(jnp.bfloat16), "fsdp", scatter_dimension=0, tiled=True
        ).astype(jnp.float32),
        lax.psum_scatter(
            gradient_feedforward_gain.astype(jnp.bfloat16), "fsdp", scatter_dimension=0, tiled=True
        ).astype(jnp.float32),
        lax.psum_scatter(
            gradient_feedforward_shift.astype(jnp.bfloat16), "fsdp", scatter_dimension=0, tiled=True
        ).astype(jnp.float32),
        lax.psum_scatter(
            grad_expand.astype(jnp.bfloat16), "fsdp", scatter_dimension=0, tiled=True
        ).astype(jnp.float32),
        lax.psum_scatter(
            grad_expand_bias.astype(jnp.bfloat16), "fsdp", scatter_dimension=0, tiled=True
        ).astype(jnp.float32),
        lax.psum_scatter(
            grad_reduce.astype(jnp.bfloat16), "fsdp", scatter_dimension=0, tiled=True
        ).astype(jnp.float32),
        lax.psum_scatter(
            grad_reduce_bias.astype(jnp.bfloat16), "fsdp", scatter_dimension=0, tiled=True
        ).astype(jnp.float32),
    )
    totals = (
        lax.psum(owned[0].astype(jnp.bfloat16), "replica").astype(jnp.float32),
        lax.psum(owned[1].astype(jnp.bfloat16), "replica").astype(jnp.float32),
        lax.psum(owned[2].astype(jnp.bfloat16), "replica").astype(jnp.float32),
        lax.psum(owned[3].astype(jnp.bfloat16), "replica").astype(jnp.float32),
        lax.psum(owned[4].astype(jnp.bfloat16), "replica").astype(jnp.float32),
        lax.psum(owned[5].astype(jnp.bfloat16), "replica").astype(jnp.float32),
        lax.psum(owned[6].astype(jnp.bfloat16), "replica").astype(jnp.float32),
        lax.psum(owned[7].astype(jnp.bfloat16), "replica").astype(jnp.float32),
        lax.psum(owned[8].astype(jnp.bfloat16), "replica").astype(jnp.float32),
        lax.psum(owned[9].astype(jnp.bfloat16), "replica").astype(jnp.float32),
    )
    return (
        layer_out,
        grad_input,
        grad_global,
        totals[0],
        totals[1],
        totals[2],
        totals[3],
        totals[4],
        totals[5],
        totals[6],
        totals[7],
        totals[8],
        totals[9],
    )


def solution(mesh):
    in_specs = (
        P(("replica", "fsdp"), None),
        P(("replica", "fsdp"), None),
        P(("replica", "fsdp"), None),
        P("replica", None),
        P("replica", None),
        P("replica", "fsdp"),
        P("fsdp"),
        P("fsdp"),
        P("fsdp", None),
        P("fsdp", None),
        P("fsdp"),
        P("fsdp"),
        P("fsdp", None),
        P("fsdp"),
        P("fsdp", None),
        P("fsdp"),
    )
    out_specs = (
        P(("replica", "fsdp"), None),
        P(("replica", "fsdp"), None),
        P(("replica", "fsdp"), None),
        P("fsdp"),
        P("fsdp"),
        P("fsdp", None),
        P("fsdp", None),
        P("fsdp"),
        P("fsdp"),
        P("fsdp", None),
        P("fsdp"),
        P("fsdp", None),
        P("fsdp"),
    )
    return jax.shard_map(body, mesh=mesh, in_specs=in_specs, out_specs=out_specs, check_vma=False)
```

profile of v0, /device:TPU:0, one launch (start us, length us, event | category | flops | bytes accessed | tf_op | source)
XLA Modules:
  0.0 805.4 jit_solution(18170484477021151799)
XLA Ops:
  14.1 7.3 all-to-all-start.1
  23.3 4.5 all-to-all-done.1
  27.8 3.6 all-to-all-start
  34.2 50.6 %all-reduce.12 = (bf16[768]{0:T(1024)(128)(2,1)S(1)}, bf16[768]{0:T(1024)(128)(2,1)S(1)}, bf16[768]{0:T(1024)(128)(2,1)S(1)}, bf16[768]{0:T(1024)(128)(2,1)S(1)}) all-reduce(bf16[768]{0:T(1024)(128)(2,1)S(1)} %dynamic-update-slice.1, bf16[768]{0:T(1024)(128)(2,1)S(1)} %dynamic-update-slice, ...), channel_id=1, replica_groups=mesh['replica'=4,'fsdp'=8] {'fsdp'}, use_global_device_ids=true, to_apply=%add.1 | all-reduce | flops 3072 | bytes 12288
  84.8 43.5 %all-gather = bf16[8,1,384]{2,1,0:T(2,128)(2,1)S(1)} all-gather(bf16[1,1,384]{2,1,0:T(2,128)(2,1)S(1)} %reshape.552), channel_id=1, replica_groups=mesh['replica'=4,'fsdp'=8] {'fsdp'}, dimensions={0}, use_global_device_ids=true | all-gather | bytes 6912 | tf_op jit(solution)/shard_map/all_gather | solution.py:134
  138.0 4.3 all-to-all-start.3
  149.5 6.3 convolution_convert_fusion
  177.7 3.9 fusion.60
  183.8 60.6 %all-gather.10.cloned.1.call-done = bf16[768,3072]{1,0:T(8,128)(2,1)} async-done(((bf16[96,3072]{1,0:T(8,128)(2,1)}), bf16[768,3072]{1,0:T(8,128)(2,1)}) %all-gather.10.cloned.1.call-update) | async-done | bytes 4718608 | tf_op jit(solution)/shard_map/all_gather | solution.py:133
  244.4 37.7 %fusion.2 = (bf16[1024,3072]{1,0:T(8,128)(2,1)}, f32[1024,3072]{1,0:T(8,128)}) fusion(f32[3072]{0:T(1024)S(1)} %bitcast.199, bf16[768,3072]{1,0:T(8,128)(2,1)} %all-gather.10.cloned.1.call-done, f32[1024,768]{1,0:T(8,128)} %copy-done.10, f32[768]{0:T(1024)S(1)} %convert_element_type.192, f32[768]{0:T(1024)S(1)} %convert_element_type.191, ...), kind=kOutput, calls=%fused_computation.12 | convolution fusion | flops 5043388416 | bytes 26765312 | tf_op jit(solution)/shard_map/dot_general | solution.py:179
  282.1 42.4 %all-gather.12.cloned.1.call-done = bf16[3072,768]{1,0:T(8,128)(2,1)} async-done(((bf16[384,768]{1,0:T(8,128)(2,1)}), bf16[3072,768]{1,0:T(8,128)(2,1)}) %all-gather.12.cloned.1.call-update) | async-done | bytes 4718608 | tf_op jit(solution)/shard_map/all_gather | solution.py:135
  324.5 12.5 %fusion.61 = (bf16[3072]{0:T(1024)(128)(2,1)S(1)}, bf16[1024,3072]{1,0:T(8,128)(2,1)S(1)}) fusion(f32[1024,3072]{1,0:T(8,128)} %get-tuple-element.60, f32[3072]{0:T(1024)S(1)} %bitcast.200, bf16[1024,768]{1,0:T(8,128)(2,1)} %bitcast.25, bf16[3072,768]{1,0:T(8,128)(2,1)} %all-gather.12.cloned.1.call-done), kind=kOutput, calls=%fused_computation.152 | convolution fusion | flops 4869583872 | bytes 25184256 | tf_op jit(solution)/shard_map/dot_general | solution.py:19
  337.1 5.7 multiply_reduce_fusion.1
  354.8 5.0 multiply_reduce_fusion
  363.4 3.5 fusion.27
  367.2 4.8 fusion.28
  374.5 5.0 fusion.29
  384.2 5.5 convolution_convert_fusion.3
  390.1 10.4 %convolution_convert_fusion.2 = bf16[768,3072]{1,0:T(8,128)(2,1)} fusion(bf16[1024,3072]{1,0:T(8,128)(2,1)} %copy-done.43, f32[1024,768]{1,0:T(8,128)} %copy-done.10, f32[768]{0:T(1024)S(1)} %convert_element_type.192, f32[768]{0:T(1024)S(1)} %convert_element_type.191, f32[1024]{0:T(1024)S(1)} %add_rsqrt_fusion, f32[1024]{0:T(1024)S(1)} %broadcast_multiply_fusion.4), kind=kOutput, calls=%fused_computation.38 | convolution fusion | flops 4838129664 | bytes 14170112 | tf_op jit(solution)/shard_map/dot_general | solution.py:13
  400.6 9.1 %convolution_convert_fusion.1 = bf16[3072,768]{1,0:T(8,128)(2,1)} fusion(bf16[1024,3072]{1,0:T(8,128)(2,1)} %get-tuple-element.59, bf16[1024,768]{1,0:T(8,128)(2,1)} %bitcast.25), kind=kOutput, calls=%fused_computation.37 | convolution fusion | flops 4834197504 | bytes 12582912 | tf_op jit(solution)/shard_map/dot_general | solution.py:13
  412.5 9.6 %multiply_reduce_fusion.2 = (bf16[768]{0:T(1024)(128)(2,1)S(1)}, f32[1024]{0:T(1024)S(1)}, f32[1024]{0:T(1024)S(1)}, bf16[768]{0:T(1024)(128)(2,1)S(1)}, f32[1024,768]{1,0:T(8,128)}) fusion(f32[1024]{0:T(1024)S(1)} %copy-done.26, f32[1024]{0:T(1024)S(1)} %copy-done.22, bf16[128,8,768]{2,1,0:T(8,128)(2,1)S(1)} %copy-done.8, ...), kind=kOutput, calls=%fused_computation.45 | convolution fusion | flops 3633312256 | bytes 14571520 | tf_op jit(solution)/shard_map/dot_general | solution.py:19
  422.1 35.5 %all-reduce.11 = (bf16[768]{0:T(1024)(128)(2,1)S(1)}, bf16[768]{0:T(1024)(128)(2,1)S(1)}, bf16[768]{0:T(1024)(128)(2,1)S(1)}, bf16[768]{0:T(1024)(128)(2,1)S(1)}...) all-reduce(bf16[768]{0:T(1024)(128)(2,1)S(1)} %dynamic-update-slice, ...), channel_id=1, replica_groups=mesh['replica'=4,'fsdp'=8] {'fsdp'}, use_global_device_ids=true, to_apply=%add.4 | all-reduce | flops 7680 | bytes 30720
  457.7 9.9 %add_convert_fusion.1 = bf16[1024,768]{1,0:T(8,128)(2,1)} fusion(f32[1024,768]{1,0:T(8,128)} %copy-done.10, bf16[1024,3072]{1,0:T(8,128)(2,1)} %get-tuple-element.59, bf16[3072,768]{1,0:T(8,128)(2,1)} %all-gather.12.cloned.1.call-done, f32[768]{0:T(1024)S(1)} %convert_element_type.196), kind=kOutput, calls=%fused_computation.53 | convolution fusion | flops 4834197504 | bytes 15731712 | tf_op jit(solution)/shard_map/dot_general | solution.py:185
  467.6 4.3 all-to-all-start.2
  471.9 4.4 add_convert_fusion
  476.4 28.1 %all-to-all-done.2 = bf16[8,128,768]{2,1,0:T(8,128)(2,1)} async-done(((bf16[8,128,768]{2,1,0:T(8,128)(2,1)}), bf16[8,128,768]{2,1,0:T(8,128)(2,1)}, u32[]{:S(2)}, u32[]{:S(2)}) %all-to-all-start.2) | async-done | bytes 1572896 | tf_op jit(solution)/shard_map/all_to_all | solution.py:188
  504.4 3.7 all-to-all-start.4
  508.2 30.2 %reduce-scatter.5.cloned.1.call-done = bf16[96,2304]{1,0:T(8,128)(2,1)} async-done(((bf16[768,2304]{1,0:T(8,128)(2,1)}), bf16[96,2304]{1,0:T(8,128)(2,1)}) %reduce-scatter.5.cloned.1.call-update) | async-done | bytes 442384 | tf_op jit(solution)/shard_map/reduce_scatter | solution.py:276
  538.4 105.4 %reduce-scatter.9.cloned.1.call-done = bf16[96,3072]{1,0:T(8,128)(2,1)} async-done(((bf16[768,3072]{1,0:T(8,128)(2,1)}), bf16[96,3072]{1,0:T(8,128)(2,1)}) %reduce-scatter.9.cloned.1.call-update) | async-done | bytes 589840 | tf_op jit(solution)/shard_map/reduce_scatter | solution.py:288
  643.8 98.9 %reduce-scatter.11.cloned.1.call-done = bf16[384,768]{1,0:T(8,128)(2,1)} async-done(((bf16[3072,768]{1,0:T(8,128)(2,1)}), bf16[384,768]{1,0:T(8,128)(2,1)}) %reduce-scatter.11.cloned.1.call-update) | async-done | bytes 589840 | tf_op jit(solution)/shard_map/reduce_scatter | solution.py:294
  745.6 6.8 all-reduce.13
  765.3 26.4 %all-reduce.17.cloned.1.call-done = (bf16[96,2304]{1,0:T(8,128)(2,1)}, bf16[96,768]{1,0:T(8,128)(2,1)}, bf16[96,3072]{1,0:T(8,128)(2,1)}, bf16[384,768]{1,0:T(8,128)(2,1)}) async-done(((bf16[96,2304]{1,0:T(8,128)(2,1)}, bf16[96,768]{1,0:T(8,128)(2,1)}, bf16[96,3072]{1,0:T(8,128)(2,1)}, bf16[384,768]{1,0:T(8,128)(2,1)}), (bf16[96,2304]{1,0:T(8,128)(2,1)}, bf16[96,768]{1,0:T(8,128)(2,1)}, ...) | async-done | bytes 1769488 | tf_op jit(solution)/shard_map/psum | solution.py:304
  (226 shorter events, 99.1 us)
Async XLA Ops:
  7.2 14.2 %copy-start = (bf16[1024,768]{1,0:T(8,128)(2,1)S(1)}, bf16[1024,768]{1,0:T(8,128)(2,1)}, u32[]{:S(2)}) copy-start(bf16[1024,768]{1,0:T(8,128)(2,1)} %param.16) | copy-start | bytes 4718596
  7.2 142.3 %all-gather.6.cloned.1.call-start = ((), (), s32[]{:S(2)}) async-start(), calls=%async_computation.9 | async-start | bytes 3981312 | tf_op jit(solution)/shard_map/all_gather | solution.py:129
  7.9 169.8 %all-gather.8.cloned.1.call-start = ((), (), s32[]{:S(2)}) async-start(), calls=%async_computation.10 | async-start | bytes 1327104 | tf_op jit(solution)/shard_map/all_gather | solution.py:130
  8.7 235.7 %all-gather.10.cloned.1.call-start = ((), (), s32[]{:S(2)}) async-start(), calls=%async_computation.11 | async-start | bytes 5308416 | tf_op jit(solution)/shard_map/all_gather | solution.py:133
  14.1 13.7 %all-to-all-start.1 = ((s32[8,16,1]{1,2,0:T(1,128)}), s32[8,16,1]{1,2,0:T(1,128)S(1)}, u32[]{:S(2)}, u32[]{:S(2)}) async-start(s32[8,16,1]{1,2,0:T(1,128)} %bitcast.11), calls=%async_computation.1 | async-start | bytes 8192 | tf_op jit(solution)/shard_map/all_to_all | solution.py:113
  21.4 10.6 %copy-start.29 = (u32[32]{0:T(128)S(1)}, u32[32]{0:T(128)}, u32[]{:S(2)}) copy-start(u32[32]{0:T(128)} %constant.168) | copy-start | bytes 388
  21.4 11.8 %copy-start.37 = (bf16[96]{0:T(256)(128)(2,1)S(1)}, bf16[96]{0:T(256)(128)(2,1)}, u32[]{:S(2)}) copy-start(bf16[96]{0:T(256)(128)(2,1)} %param.23) | copy-start | bytes 580
  21.4 12.1 %copy-start.38 = (bf16[96]{0:T(256)(128)(2,1)S(1)}, bf16[96]{0:T(256)(128)(2,1)}, u32[]{:S(2)}) copy-start(bf16[96]{0:T(256)(128)(2,1)} %param.22) | copy-start | bytes 580
  21.5 12.3 %copy-start.39 = (bf16[96]{0:T(256)(128)(2,1)S(1)}, bf16[96]{0:T(256)(128)(2,1)}, u32[]{:S(2)}) copy-start(bf16[96]{0:T(256)(128)(2,1)} %param.27) | copy-start | bytes 580
  21.5 12.5 %copy-start.40 = (bf16[96]{0:T(256)(128)(2,1)S(1)}, bf16[96]{0:T(256)(128)(2,1)}, u32[]{:S(2)}) copy-start(bf16[96]{0:T(256)(128)(2,1)} %param.26) | copy-start | bytes 580
  21.5 63.3 %copy-start.30 = (bf16[384]{0:T(512)(128)(2,1)S(1)}, bf16[384]{0:T(512)(128)(2,1)}, u32[]{:S(2)}) copy-start(bf16[384]{0:T(512)(128)(2,1)} %param.29) | copy-start | bytes 2308
  21.5 106.8 %copy-start.41 = (s32[1,4]{1,0:T(1,128)S(1)}, s32[1,4]{1,0:T(1,128)}, u32[]{:S(2)}) copy-start(s32[1,4]{1,0:T(1,128)} %param.19) | copy-start | bytes 52
  21.5 107.1 %copy-start.31 = (s32[1,4]{1,0:T(1,128)S(1)}, s32[1,4]{1,0:T(1,128)}, u32[]{:S(2)}) copy-start(s32[1,4]{1,0:T(1,128)} %param.20) | copy-start | bytes 52
  27.8 110.2 %all-to-all-start = ((bf16[8,128,768]{2,1,0:T(8,128)(2,1)}), bf16[8,128,768]{2,1,0:T(8,128)(2,1)S(1)}, u32[]{:S(2)}, u32[]{:S(2)}) async-start(bf16[8,128,768]{2,1,0:T(8,128)(2,1)} %bitcast.8), calls=%async_computation | async-start | bytes 3145728 | tf_op jit(solution)/shard_map/all_to_all | solution.py:112
  31.4 293.1 %all-gather.12.cloned.1.call-start = ((), (), s32[]{:S(2)}) async-start(), calls=%async_computation.12 | async-start | bytes 5308416 | tf_op jit(solution)/shard_map/all_gather | solution.py:135
  84.8 61.1 %copy-start.23 = (f32[768]{0:T(1024)}, f32[768]{0:T(1024)S(1)}, u32[]{:S(2)}) copy-start(f32[768]{0:T(1024)S(1)} %convert_element_type.183) | copy-start | bytes 9220
  135.9 10.0 %copy-start.7 = (bf16[128,8,768]{2,1,0:T(8,128)(2,1)}, bf16[128,8,768]{2,1,0:T(8,128)(2,1)S(1)}, u32[]{:S(2)}) copy-start(bf16[128,8,768]{2,1,0:T(8,128)(2,1)S(1)} %gather_fusion.2) | copy-start | bytes 4718596
  138.0 7.9 copy-start.3
  138.0 144.1 %all-to-all-start.3 = ((bf16[8,128,768]{2,1,0:T(8,128)(2,1)}), bf16[8,128,768]{2,1,0:T(8,128)(2,1)}, u32[]{:S(2)}, u32[]{:S(2)}) async-start(bf16[8,128,768]{2,1,0:T(8,128)(2,1)} %bitcast.186), calls=%async_computation.3 | async-start | bytes 3145728 | tf_op jit(solution)/shard_map/all_to_all | solution.py:193
  142.3 365.8 %reduce-scatter.7.cloned.1.call-start = ((), (), s32[]{:S(2)}) async-start(), calls=%async_computation.14 | async-start | bytes 1327104 | tf_op jit(solution)/shard_map/reduce_scatter | solution.py:279
  324.5 12.5 %copy-start.11 = (f32[1024,768]{1,0:T(8,128)S(1)}, f32[1024,768]{1,0:T(8,128)}, u32[]{:S(2)}) copy-start(f32[1024,768]{1,0:T(8,128)} %copy-done.10) | copy-start | bytes 9437188
  324.5 12.6 %copy-start.35 = (bf16[768,3072]{1,0:T(8,128)(2,1)S(1)}, bf16[768,3072]{1,0:T(8,128)(2,1)}, u32[]{:S(2)}) copy-start(bf16[768,3072]{1,0:T(8,128)(2,1)} %all-gather.10.cloned.1.call-done) | copy-start | bytes 14155780
  353.8 5.9 slice-start
  367.0 171.4 %reduce-scatter.5.cloned.1.call-start = ((), (), s32[]{:S(2)}) async-start(), calls=%async_computation.13 | async-start | bytes 3981312 | tf_op jit(solution)/shard_map/reduce_scatter | solution.py:276
  389.7 254.1 %reduce-scatter.9.cloned.1.call-start = ((), (), s32[]{:S(2)}) async-start(), calls=%async_computation.15 | async-start | bytes 5308416 | tf_op jit(solution)/shard_map/reduce_scatter | solution.py:288
  400.6 342.1 %reduce-scatter.11.cloned.1.call-start = ((), (), s32[]{:S(2)}) async-start(), calls=%async_computation.16 | async-start | bytes 5308416 | tf_op jit(solution)/shard_map/reduce_scatter | solution.py:294
  467.6 36.8 %all-to-all-start.2 = ((bf16[8,128,768]{2,1,0:T(8,128)(2,1)}), bf16[8,128,768]{2,1,0:T(8,128)(2,1)}, u32[]{:S(2)}, u32[]{:S(2)}) async-start(bf16[8,128,768]{2,1,0:T(8,128)(2,1)} %bitcast.195), calls=%async_computation.2 | async-start | bytes 3145728 | tf_op jit(solution)/shard_map/all_to_all | solution.py:188
  476.3 267.6 %copy-start.33 = (s32[128]{0:T(128)S(1)}, s32[128]{0:T(128)}, u32[]{:S(2)}) copy-start(s32[128]{0:T(128)} %copy-done.32) | copy-start | bytes 1540
  476.3 279.2 %copy-start.9 = (bf16[1024,768]{1,0:T(8,128)(2,1)S(1)}, bf16[1024,768]{1,0:T(8,128)(2,1)}, u32[]{:S(2)}) copy-start(bf16[1024,768]{1,0:T(8,128)(2,1)} %add_convert_fusion) | copy-start | bytes 4718596
  504.4 256.2 %all-to-all-start.4 = ((bf16[8,128,768]{2,1,0:T(8,128)(2,1)}), bf16[8,128,768]{2,1,0:T(8,128)(2,1)S(1)}, u32[]{:S(2)}, u32[]{:S(2)}) async-start(bf16[8,128,768]{2,1,0:T(8,128)(2,1)} %bitcast.174), calls=%async_computation.4 | async-start | bytes 3145728 | tf_op jit(solution)/shard_map/all_to_all | solution.py:267
  508.1 283.6 %all-reduce.17.cloned.1.call-start = ((), (), s32[]{:S(2)}) async-start(), calls=%async_computation.17 | async-start | bytes 3538944 | tf_op jit(solution)/shard_map/psum | solution.py:304
  762.4 36.2 %copy-start.1 = (bf16[1024,768]{1,0:T(8,128)(2,1)S(1)}, bf16[1024,768]{1,0:T(8,128)(2,1)}, u32[]{:S(2)}) copy-start(bf16[1024,768]{1,0:T(8,128)(2,1)} %param.16) | copy-start | bytes 4718596
  (28 other events, 79.8 us)
Sparse Core Ops, SparseCore 0:
  10.2 92.3 all-gather.5
  104.8 45.2 all-gather.7
  152.3 92.0 all-gather.9
  246.4 78.0 all-gather.11
  367.1 62.1 reduce-scatter.6
  432.8 105.5 reduce-scatter.4
  542.0 101.7 reduce-scatter.8
  647.4 95.2 reduce-scatter.10
  745.3 46.3 all-reduce.16
where the time goes:
time: 813 us; the launch traced here: 805 us
  waiting for transfers between devices  399 us (49%)
  matrix products  137 us (17%)
  blocking collectives  136 us (17%)
  local copies, waits for them, and re-layouts  52.6 us (6%)
  other arithmetic  38.7 us (5%)
  starting transfers between devices  24.1 us (3%)
  between operations  16.9 us (2%)
    reduce_scatter x1, waiting for transfers between devices, body(): lax.psum_scatter(grad_expand.astype(jnp.bfloat16), 'fsdp', scatter_dimens...  105 us
    reduce_scatter x1, waiting for transfers between devices, body(): lax.psum_scatter(grad_reduce.astype(jnp.bfloat16), 'fsdp', scatter_dimens...  98.9 us
    unnamed x2, blocking collectives  86.1 us
    all_gather x1, waiting for transfers between devices, body(): lax.all_gather(up_weight, 'fsdp', axis=0, tiled=True)  60.6 us
    all_gather x1, blocking collectives, body(): lax.all_gather(up_bias, 'fsdp', axis=0, tiled=True)  43.5 us
    all_gather x1, waiting for transfers between devices, body(): lax.all_gather(down_weight, 'fsdp', axis=0, tiled=True)  42.4 us
    dot_general x1, matrix products, body(): jnp.dot(second_in, expand_full, preferred_element_type=jnp.float32)  37.7 us
    dot_general x4, matrix products, contract_cols(): lax.dot_general(left, right, (((1,), (1,)), ((), ())), preferred_element_...  31.2 us
  transfers between devices with their start and end apart: 14, of which 8 were waited for; matrix products, arithmetic and copies ran while one was open for 21% of the time, Pallas kernels for 0%

commit v1 on v0

--- a/solution.py
+++ b/solution.py
@@ -185,9 +185,20 @@
         + jnp.dot(activ, reduce_full, preferred_element_type=jnp.float32)
         + reduce_bias.astype(jnp.float32)
     )
-    returned = lax.all_to_all(
-        result.astype(jnp.bfloat16), "fsdp", split_axis=0, concat_axis=0, tiled=True
-    )
+    value = result.astype(jnp.bfloat16)
+    ways, here = (lax.axis_size("fsdp"), lax.axis_index("fsdp"))
+    width = value.shape[0] // ways
+    lengths = list(value.shape)
+    lengths[0] = width
+    height = lengths[0]
+    lengths[0] = height * ways
+    full = jnp.zeros(lengths, value.dtype)
+    for mask in range(ways):
+        part = lax.dynamic_slice_in_dim(value, (here ^ mask) * width, width, axis=0)
+        if mask:
+            part = lax.ppermute(part, "fsdp", [(d, d ^ mask) for d in range(ways)])
+        full = lax.dynamic_update_slice_in_dim(full, part, (here ^ mask) * height, axis=0)
+    returned = full
     layer_out = jnp.where(keep_byte, unpack_rows(returned), jnp.zeros((), jnp.bfloat16))
     masked_cot = jnp.where(keep_byte, cotangent, jnp.zeros((), jnp.bfloat16))
     upstream_b = lax.all_to_all(

time: 813 us -> 811 us (level)
  waiting for transfers between devices: 399 us -> 374 us
  local copies, waits for them, and re-layouts: 52.6 us -> 67.8 us
    all_to_all x1 -> x0, waiting for transfers between devices: 28.1 us -> none  [body(): lax.all_to_all(result.astype(jnp.bfloat16), 'fsdp', split_axis=0, concat_...]
    ppermute x0 -> x7, starting transfers between devices: none -> 11.1 us  [body(): part = lax.ppermute(part, 'fsdp', [(d, d ^ mask) for d in range(ways)])]
    psum x1, waiting for transfers between devices: 26.4 us -> 37.5 us  [body(): lax.psum(owned[2].astype(jnp.bfloat16), 'replica').astype(jnp.float32)]
    dynamic_update_slice x0 -> x7, local copies, waits for them, and re-layouts: none -> 9.48 us  [body(): lax.dynamic_update_slice_in_dim(full, part, (here ^ mask) * height, axis=0)]
    reduce_scatter x1, waiting for transfers between devices: 105 us -> 97.3 us  [body(): lax.psum_scatter(grad_expand.astype(jnp.bfloat16), 'fsdp', scatter_dimens...]
  transfers between devices with their start and end apart: 14 -> 20, of which waited for: 8 -> 7; matrix products, arithmetic and copies ran while one was open for 21% -> 23% of each run, Pallas kernels for 0% -> 0%
where the time goes in v1:
time: 811 us; the launch traced here: 803 us
  waiting for transfers between devices  374 us (46%)
  blocking collectives  137 us (17%)
  matrix products  137 us (17%)
  local copies, waits for them, and re-layouts  67.8 us (8%)
  other arithmetic  40.3 us (5%)
  starting transfers between devices  30.9 us (4%)
  between operations  17.3 us (2%)
    reduce_scatter x1, waiting for transfers between devices, body(): lax.psum_scatter(grad_reduce.astype(jnp.bfloat16), 'fsdp', scatter_dimens...  98.8 us
    reduce_scatter x1, waiting for transfers between devices, body(): lax.psum_scatter(grad_expand.astype(jnp.bfloat16), 'fsdp', scatter_dimens...  97.3 us
    unnamed x2, blocking collectives  86.4 us
    all_gather x1, waiting for transfers between devices, body(): lax.all_gather(up_weight, 'fsdp', axis=0, tiled=True)  60.6 us
    all_gather x1, blocking collectives, body(): lax.all_gather(up_bias, 'fsdp', axis=0, tiled=True)  43.4 us
    all_gather x1, waiting for transfers between devices, body(): lax.all_gather(down_weight, 'fsdp', axis=0, tiled=True)  42.3 us
    dot_general x1, matrix products, body(): jnp.dot(second_in, expand_full, preferred_element_type=jnp.float32)  37.8 us
    psum x1, waiting for transfers between devices, body(): lax.psum(owned[2].astype(jnp.bfloat16), 'replica').astype(jnp.float32)  37.5 us
  transfers between devices with their start and end apart: 20, of which 7 were waited for; matrix products, arithmetic and copies ran while one was open for 23% of the time, Pallas kernels for 0%

profile of v1, /device:TPU:0, one launch (start us, length us, event | category | flops | bytes accessed | tf_op | source)
XLA Modules:
  0.0 803.4 jit_solution(9091327388441003567)
XLA Ops:
  14.1 7.3 all-to-all-start.1
  23.3 4.5 all-to-all-done.1
  27.8 3.6 all-to-all-start
  34.2 50.6 %all-reduce.12 = (bf16[768]{0:T(1024)(128)(2,1)S(1)}, bf16[768]{0:T(1024)(128)(2,1)S(1)}, bf16[768]{0:T(1024)(128)(2,1)S(1)}, bf16[768]{0:T(1024)(128)(2,1)S(1)}) all-reduce(bf16[768]{0:T(1024)(128)(2,1)S(1)} %dynamic-update-slice.1, bf16[768]{0:T(1024)(128)(2,1)S(1)} %dynamic-update-slice, ...), channel_id=1, replica_groups=mesh['replica'=4,'fsdp'=8] {'fsdp'}, use_global_device_ids=true, to_apply=%add.1 | all-reduce | flops 3072 | bytes 12288
  84.8 43.4 %all-gather = bf16[8,1,384]{2,1,0:T(2,128)(2,1)S(1)} all-gather(bf16[1,1,384]{2,1,0:T(2,128)(2,1)S(1)} %reshape.549), channel_id=1, replica_groups=mesh['replica'=4,'fsdp'=8] {'fsdp'}, dimensions={0}, use_global_device_ids=true | all-gather | bytes 6912 | tf_op jit(solution)/shard_map/all_gather | solution.py:134
  138.0 4.3 all-to-all-start.2
  149.4 6.3 convolution_convert_fusion
  177.7 3.9 fusion.60
  183.7 60.6 %all-gather.10.cloned.1.call-done = bf16[768,3072]{1,0:T(8,128)(2,1)} async-done(((bf16[96,3072]{1,0:T(8,128)(2,1)}), bf16[768,3072]{1,0:T(8,128)(2,1)}) %all-gather.10.cloned.1.call-update) | async-done | bytes 4718608 | tf_op jit(solution)/shard_map/all_gather | solution.py:133
  244.4 37.8 %fusion.2 = (bf16[1024,3072]{1,0:T(8,128)(2,1)}, f32[1024,3072]{1,0:T(8,128)}) fusion(f32[3072]{0:T(1024)S(1)} %bitcast.197, bf16[768,3072]{1,0:T(8,128)(2,1)} %all-gather.10.cloned.1.call-done, f32[1024,768]{1,0:T(8,128)} %copy-done.10, f32[768]{0:T(1024)S(1)} %convert_element_type.192, f32[768]{0:T(1024)S(1)} %convert_element_type.191, ...), kind=kOutput, calls=%fused_computation.12 | convolution fusion | flops 5043388416 | bytes 26765312 | tf_op jit(solution)/shard_map/dot_general | solution.py:179
  282.1 42.3 %all-gather.12.cloned.1.call-done = bf16[3072,768]{1,0:T(8,128)(2,1)} async-done(((bf16[384,768]{1,0:T(8,128)(2,1)}), bf16[3072,768]{1,0:T(8,128)(2,1)}) %all-gather.12.cloned.1.call-update) | async-done | bytes 4718608 | tf_op jit(solution)/shard_map/all_gather | solution.py:135
  324.5 12.5 %fusion.61 = (bf16[3072]{0:T(1024)(128)(2,1)S(1)}, bf16[1024,3072]{1,0:T(8,128)(2,1)S(1)}) fusion(f32[1024,3072]{1,0:T(8,128)} %get-tuple-element.68, f32[3072]{0:T(1024)S(1)} %bitcast.198, bf16[1024,768]{1,0:T(8,128)(2,1)} %bitcast.24, bf16[3072,768]{1,0:T(8,128)(2,1)} %all-gather.12.cloned.1.call-done), kind=kOutput, calls=%fused_computation.167 | convolution fusion | flops 4869583872 | bytes 25184256 | tf_op jit(solution)/shard_map/dot_general | solution.py:19
  337.0 5.7 multiply_reduce_fusion.1
  349.2 3.3 convolution_convert_fusion.4
  354.7 5.0 multiply_reduce_fusion
  363.4 3.5 fusion.27
  367.2 4.8 fusion.28
  374.4 5.0 fusion.29
  384.0 5.4 convolution_convert_fusion.3
  390.0 10.5 %convolution_convert_fusion.2 = bf16[768,3072]{1,0:T(8,128)(2,1)} fusion(bf16[1024,3072]{1,0:T(8,128)(2,1)} %copy-done.43, f32[1024,768]{1,0:T(8,128)} %copy-done.10, f32[768]{0:T(1024)S(1)} %convert_element_type.192, f32[768]{0:T(1024)S(1)} %convert_element_type.191, f32[1024]{0:T(1024)S(1)} %add_rsqrt_fusion, f32[1024]{0:T(1024)S(1)} %broadcast_multiply_fusion.4), kind=kOutput, calls=%fused_computation.38 | convolution fusion | flops 4838129664 | bytes 14170112 | tf_op jit(solution)/shard_map/dot_general | solution.py:13
  400.6 9.2 %convolution_convert_fusion.1 = bf16[3072,768]{1,0:T(8,128)(2,1)} fusion(bf16[1024,3072]{1,0:T(8,128)(2,1)} %get-tuple-element.67, bf16[1024,768]{1,0:T(8,128)(2,1)} %bitcast.24), kind=kOutput, calls=%fused_computation.37 | convolution fusion | flops 4834197504 | bytes 12582912 | tf_op jit(solution)/shard_map/dot_general | solution.py:13
  414.6 9.8 %multiply_reduce_fusion.2 = (bf16[768]{0:T(1024)(128)(2,1)S(1)}, f32[1024]{0:T(1024)S(1)}, f32[1024]{0:T(1024)S(1)}, bf16[768]{0:T(1024)(128)(2,1)S(1)}, f32[1024,768]{1,0:T(8,128)}) fusion(f32[1024]{0:T(1024)S(1)} %copy-done.26, f32[1024]{0:T(1024)S(1)} %copy-done.22, bf16[128,8,768]{2,1,0:T(8,128)(2,1)S(1)} %copy-done.8, ...), kind=kOutput, calls=%fused_computation.45 | convolution fusion | flops 3633312256 | bytes 14571520 | tf_op jit(solution)/shard_map/dot_general | solution.py:19
  424.3 35.8 %all-reduce.11 = (bf16[768]{0:T(1024)(128)(2,1)S(1)}, bf16[768]{0:T(1024)(128)(2,1)}, bf16[768]{0:T(1024)(128)(2,1)}, bf16[768]{0:T(1024)(128)(2,1)}, bf16[768]{...) all-reduce(bf16[768]{0:T(1024)(128)(2,1)S(1)} %dynamic-update-slice, ...), channel_id=1, replica_groups=mesh['replica'=4,'fsdp'=8] {'fsdp'}, use_global_device_ids=true, to_apply=%add.4 | all-reduce | flops 7680 | bytes 30720
  460.2 4.5 add_convert_fusion
  464.6 3.6 all-to-all-start.3
  468.3 9.1 %add_convert_fusion.1 = bf16[1024,768]{1,0:T(8,128)(2,1)S(1)} fusion(f32[1024,768]{1,0:T(8,128)} %copy-done.10, bf16[1024,3072]{1,0:T(8,128)(2,1)} %get-tuple-element.67, bf16[3072,768]{1,0:T(8,128)(2,1)} %all-gather.12.cloned.1.call-done, f32[768]{0:T(1024)S(1)} %convert_element_type.196), kind=kOutput, calls=%fused_computation.53 | convolution fusion | flops 4834197504 | bytes 15731712 | tf_op jit(solution)/shard_map/dot_general | solution.py:185
  493.1 6.7 all-reduce.13
  508.0 3.3 collective-permute-start.5
  514.7 29.9 %reduce-scatter.5.cloned.1.call-done = bf16[96,2304]{1,0:T(8,128)(2,1)} async-done(((bf16[768,2304]{1,0:T(8,128)(2,1)}), bf16[96,2304]{1,0:T(8,128)(2,1)}) %reduce-scatter.5.cloned.1.call-update) | async-done | bytes 442384 | tf_op jit(solution)/shard_map/reduce_scatter | solution.py:287
  544.6 97.3 %reduce-scatter.9.cloned.1.call-done = bf16[96,3072]{1,0:T(8,128)(2,1)} async-done(((bf16[768,3072]{1,0:T(8,128)(2,1)}), bf16[96,3072]{1,0:T(8,128)(2,1)}) %reduce-scatter.9.cloned.1.call-update) | async-done | bytes 589840 | tf_op jit(solution)/shard_map/reduce_scatter | solution.py:299
  641.9 98.8 %reduce-scatter.11.cloned.1.call-done = bf16[384,768]{1,0:T(8,128)(2,1)} async-done(((bf16[3072,768]{1,0:T(8,128)(2,1)}), bf16[384,768]{1,0:T(8,128)(2,1)}) %reduce-scatter.11.cloned.1.call-update) | async-done | bytes 589840 | tf_op jit(solution)/shard_map/reduce_scatter | solution.py:305
  752.2 37.5 %all-reduce.17.cloned.1.call-done = (bf16[96,2304]{1,0:T(8,128)(2,1)}, bf16[96,768]{1,0:T(8,128)(2,1)}, bf16[96,3072]{1,0:T(8,128)(2,1)}, bf16[384,768]{1,0:T(8,128)(2,1)}) async-done(((bf16[96,2304]{1,0:T(8,128)(2,1)}, bf16[96,768]{1,0:T(8,128)(2,1)}, bf16[96,3072]{1,0:T(8,128)(2,1)}, bf16[384,768]{1,0:T(8,128)(2,1)}), (bf16[96,2304]{1,0:T(8,128)(2,1)}, bf16[96,768]{1,0:T(8,128)(2,1)}, ...) | async-done | bytes 1769488 | tf_op jit(solution)/shard_map/psum | solution.py:315
  (247 shorter events, 120.3 us)
Async XLA Ops:
  7.2 14.2 %copy-start = (bf16[1024,768]{1,0:T(8,128)(2,1)S(1)}, bf16[1024,768]{1,0:T(8,128)(2,1)}, u32[]{:S(2)}) copy-start(bf16[1024,768]{1,0:T(8,128)(2,1)} %param.16) | copy-start | bytes 4718596
  7.2 142.2 %all-gather.6.cloned.1.call-start = ((), (), s32[]{:S(2)}) async-start(), calls=%async_computation.8 | async-start | bytes 3981312 | tf_op jit(solution)/shard_map/all_gather | solution.py:129
  7.9 169.8 %all-gather.8.cloned.1.call-start = ((), (), s32[]{:S(2)}) async-start(), calls=%async_computation.9 | async-start | bytes 1327104 | tf_op jit(solution)/shard_map/all_gather | solution.py:130
  8.7 235.7 %all-gather.10.cloned.1.call-start = ((), (), s32[]{:S(2)}) async-start(), calls=%async_computation.10 | async-start | bytes 5308416 | tf_op jit(solution)/shard_map/all_gather | solution.py:133
  11.2 16.6 %copy-start.32 = (s32[128]{0:T(128)}, s32[128]{0:T(128)S(1)}, u32[]{:S(2)}) copy-start(s32[128]{0:T(128)S(1)} %fusion.49) | copy-start | bytes 1540
  14.1 13.7 %all-to-all-start.1 = ((s32[8,16,1]{1,2,0:T(1,128)}), s32[8,16,1]{1,2,0:T(1,128)S(1)}, u32[]{:S(2)}, u32[]{:S(2)}) async-start(s32[8,16,1]{1,2,0:T(1,128)} %bitcast.11), calls=%async_computation.1 | async-start | bytes 8192 | tf_op jit(solution)/shard_map/all_to_all | solution.py:113
  21.5 12.3 %copy-start.39 = (bf16[96]{0:T(256)(128)(2,1)S(1)}, bf16[96]{0:T(256)(128)(2,1)}, u32[]{:S(2)}) copy-start(bf16[96]{0:T(256)(128)(2,1)} %param.27) | copy-start | bytes 580
  21.5 12.5 %copy-start.40 = (bf16[96]{0:T(256)(128)(2,1)S(1)}, bf16[96]{0:T(256)(128)(2,1)}, u32[]{:S(2)}) copy-start(bf16[96]{0:T(256)(128)(2,1)} %param.26) | copy-start | bytes 580
  21.5 63.3 %copy-start.30 = (bf16[384]{0:T(512)(128)(2,1)S(1)}, bf16[384]{0:T(512)(128)(2,1)}, u32[]{:S(2)}) copy-start(bf16[384]{0:T(512)(128)(2,1)} %param.29) | copy-start | bytes 2308
  21.5 106.8 %copy-start.41 = (s32[1,4]{1,0:T(1,128)S(1)}, s32[1,4]{1,0:T(1,128)}, u32[]{:S(2)}) copy-start(s32[1,4]{1,0:T(1,128)} %param.19) | copy-start | bytes 52
  21.5 107.1 %copy-start.31 = (s32[1,4]{1,0:T(1,128)S(1)}, s32[1,4]{1,0:T(1,128)}, u32[]{:S(2)}) copy-start(s32[1,4]{1,0:T(1,128)} %param.20) | copy-start | bytes 52
  27.8 110.2 %all-to-all-start = ((bf16[8,128,768]{2,1,0:T(8,128)(2,1)}), bf16[8,128,768]{2,1,0:T(8,128)(2,1)S(1)}, u32[]{:S(2)}, u32[]{:S(2)}) async-start(bf16[8,128,768]{2,1,0:T(8,128)(2,1)} %bitcast.8), calls=%async_computation | async-start | bytes 3145728 | tf_op jit(solution)/shard_map/all_to_all | solution.py:112
  31.4 293.1 %all-gather.12.cloned.1.call-start = ((), (), s32[]{:S(2)}) async-start(), calls=%async_computation.11 | async-start | bytes 5308416 | tf_op jit(solution)/shard_map/all_gather | solution.py:135
  84.8 61.1 %copy-start.23 = (f32[768]{0:T(1024)}, f32[768]{0:T(1024)S(1)}, u32[]{:S(2)}) copy-start(f32[768]{0:T(1024)S(1)} %convert_element_type.183) | copy-start | bytes 9220
  138.0 144.2 %all-to-all-start.2 = ((bf16[8,128,768]{2,1,0:T(8,128)(2,1)}), bf16[8,128,768]{2,1,0:T(8,128)(2,1)}, u32[]{:S(2)}, u32[]{:S(2)}) async-start(bf16[8,128,768]{2,1,0:T(8,128)(2,1)} %bitcast.185), calls=%async_computation.2 | async-start | bytes 3145728 | tf_op jit(solution)/shard_map/all_to_all | solution.py:204
  142.3 372.4 %reduce-scatter.7.cloned.1.call-start = ((), (), s32[]{:S(2)}) async-start(), calls=%async_computation.13 | async-start | bytes 1327104 | tf_op jit(solution)/shard_map/reduce_scatter | solution.py:290
  324.5 12.5 %copy-start.11 = (f32[1024,768]{1,0:T(8,128)S(1)}, f32[1024,768]{1,0:T(8,128)}, u32[]{:S(2)}) copy-start(f32[1024,768]{1,0:T(8,128)} %copy-done.10) | copy-start | bytes 9437188
  324.5 12.6 %copy-start.35 = (bf16[768,3072]{1,0:T(8,128)(2,1)S(1)}, bf16[768,3072]{1,0:T(8,128)(2,1)}, u32[]{:S(2)}) copy-start(bf16[768,3072]{1,0:T(8,128)(2,1)} %all-gather.10.cloned.1.call-done) | copy-start | bytes 14155780
  366.9 177.7 %reduce-scatter.5.cloned.1.call-start = ((), (), s32[]{:S(2)}) async-start(), calls=%async_computation.12 | async-start | bytes 3981312 | tf_op jit(solution)/shard_map/reduce_scatter | solution.py:287
  389.5 252.3 %reduce-scatter.9.cloned.1.call-start = ((), (), s32[]{:S(2)}) async-start(), calls=%async_computation.14 | async-start | bytes 5308416 | tf_op jit(solution)/shard_map/reduce_scatter | solution.py:299
  400.5 340.2 %reduce-scatter.11.cloned.1.call-start = ((), (), s32[]{:S(2)}) async-start(), calls=%async_computation.15 | async-start | bytes 5308416 | tf_op jit(solution)/shard_map/reduce_scatter | solution.py:305
  464.6 285.8 %all-to-all-start.3 = ((bf16[8,128,768]{2,1,0:T(8,128)(2,1)}), bf16[8,128,768]{2,1,0:T(8,128)(2,1)S(1)}, u32[]{:S(2)}, u32[]{:S(2)}) async-start(bf16[8,128,768]{2,1,0:T(8,128)(2,1)} %bitcast.173), calls=%async_computation.3 | async-start | bytes 3145728 | tf_op jit(solution)/shard_map/all_to_all | solution.py:278
  468.2 321.5 %all-reduce.17.cloned.1.call-start = ((), (), s32[]{:S(2)}) async-start(), calls=%async_computation.16 | async-start | bytes 3538944 | tf_op jit(solution)/shard_map/psum | solution.py:315
  477.4 28.7 %copy-start.9 = (bf16[1024,768]{1,0:T(8,128)(2,1)S(1)}, bf16[1024,768]{1,0:T(8,128)(2,1)}, u32[]{:S(2)}) copy-start(bf16[1024,768]{1,0:T(8,128)(2,1)} %add_convert_fusion) | copy-start | bytes 4718596
  479.7 28.3 %collective-permute-start = (bf16[128,768]{1,0:T(8,128)(2,1)}, bf16[128,768]{1,0:T(8,128)(2,1)}, u32[]{:S(2)}, u32[]{:S(2)}) collective-permute-start(bf16[128,768]{1,0:T(8,128)(2,1)} %get-tuple-element.55), channel_id=1, source_target_pairs={{0,1},{1,0},{2,3},{3,2},{4,5},{5,4},{6,7},{7,6},{8,9},{9,8},{10,11... | collective-permute-start | bytes 589832 | tf_op jit(solution)/shard_map/ppermute | solution.py:199
  481.5 31.4 %collective-permute-start.1 = (bf16[128,768]{1,0:T(8,128)(2,1)}, bf16[128,768]{1,0:T(8,128)(2,1)}, u32[]{:S(2)}, u32[]{:S(2)}) collective-permute-start(bf16[128,768]{1,0:T(8,128)(2,1)} %get-tuple-element.54), channel_id=1, source_target_pairs={{0,2},{1,3},{2,0},{3,1},{4,6},{5,7},{6,4},{7,5},{8,10},{9,11},{10,... | collective-permute-start | bytes 589832 | tf_op jit(solution)/shard_map/ppermute | solution.py:199
  483.0 257.7 %collective-permute-start.2 = (bf16[128,768]{1,0:T(8,128)(2,1)}, bf16[128,768]{1,0:T(8,128)(2,1)}, u32[]{:S(2)}, u32[]{:S(2)}) collective-permute-start(bf16[128,768]{1,0:T(8,128)(2,1)} %get-tuple-element.53), channel_id=1, source_target_pairs={{0,3},{1,2},{2,1},{3,0},{4,7},{5,6},{6,5},{7,4},{8,11},{9,10},{10,... | collective-permute-start | bytes 589832 | tf_op jit(solution)/shard_map/ppermute | solution.py:199
  483.2 259.2 %collective-permute-start.3 = (bf16[128,768]{1,0:T(8,128)(2,1)}, bf16[128,768]{1,0:T(8,128)(2,1)}, u32[]{:S(2)}, u32[]{:S(2)}) collective-permute-start(bf16[128,768]{1,0:T(8,128)(2,1)} %get-tuple-element.52), channel_id=1, source_target_pairs={{0,4},{1,5},{2,6},{3,7},{4,0},{5,1},{6,2},{7,3},{8,12},{9,13},{10,... | collective-permute-start | bytes 589832 | tf_op jit(solution)/shard_map/ppermute | solution.py:199
  485.9 258.0 %collective-permute-start.4 = (bf16[128,768]{1,0:T(8,128)(2,1)}, bf16[128,768]{1,0:T(8,128)(2,1)}, u32[]{:S(2)}, u32[]{:S(2)}) collective-permute-start(bf16[128,768]{1,0:T(8,128)(2,1)} %get-tuple-element.51), channel_id=1, source_target_pairs={{0,5},{1,4},{2,7},{3,6},{4,1},{5,0},{6,3},{7,2},{8,13},{9,12},{10,... | collective-permute-start | bytes 589832 | tf_op jit(solution)/shard_map/ppermute | solution.py:199
  508.0 237.6 %collective-permute-start.5 = (bf16[128,768]{1,0:T(8,128)(2,1)S(1)}, bf16[128,768]{1,0:T(8,128)(2,1)S(1)}, u32[]{:S(2)}, u32[]{:S(2)}) collective-permute-start(bf16[128,768]{1,0:T(8,128)(2,1)S(1)} %get-tuple-element.50), channel_id=1, source_target_pairs={{0,6},{1,7},{2,4},{3,5},{4,2},{5,3},{6,0},{7,1},{8,14},{9,15},{10,... | collective-permute-start | bytes 589832 | tf_op jit(solution)/shard_map/ppermute | solution.py:199
  512.9 233.4 %collective-permute-start.6 = (bf16[128,768]{1,0:T(8,128)(2,1)S(1)}, bf16[128,768]{1,0:T(8,128)(2,1)S(1)}, u32[]{:S(2)}, u32[]{:S(2)}) collective-permute-start(bf16[128,768]{1,0:T(8,128)(2,1)S(1)} %get-tuple-element.49), channel_id=1, source_target_pairs={{0,7},{1,6},{2,5},{3,4},{4,3},{5,2},{6,1},{7,0},{8,15},{9,14},{10,... | collective-permute-start | bytes 589832 | tf_op jit(solution)/shard_map/ppermute | solution.py:199
  750.4 46.2 %copy-start.1 = (bf16[1024,768]{1,0:T(8,128)(2,1)S(1)}, bf16[1024,768]{1,0:T(8,128)(2,1)}, u32[]{:S(2)}) copy-start(bf16[1024,768]{1,0:T(8,128)(2,1)} %param.16) | copy-start | bytes 4718596
  (34 other events, 153.6 us)
Sparse Core Ops, SparseCore 0:
  10.2 92.3 all-gather.5
  104.8 45.4 all-gather.7
  152.4 91.8 all-gather.9
  246.4 78.0 all-gather.11
  367.0 62.1 reduce-scatter.6
  432.7 111.8 reduce-scatter.4
  548.2 93.5 reduce-scatter.8
  645.5 95.1 reduce-scatter.10
  743.3 46.3 all-reduce.16
